TPU v7x, 32 devices: a whole 2x2x4 slice. The times are simulated.
32 devices in a mesh: energy: 2 (over x), mom: 16 (over z, y, core).
Axes of the slice: x: 2, y: 2, z: 4, core: 2. Of those that a mesh axis runs over, the one named last changes fastest.
Arguments:
- source: float32 [256, 128, 1024], P(('energy', 'mom')), parts along dimension 0, may hold values from -6 to 6
- green: float32 [256, 1024], P(('energy', 'mom')), parts along dimension 0, may hold values from 0.1 to 0.6
- couple_one: float32 [2, 4, 128, 128], replicated, may hold values from -0.5 to 0.5
- couple_two: float32 [2, 4, 128, 128], replicated, may hold values from -0.5 to 0.5
- p_bracket: int32 [2, 1024], replicated, may hold values from 0 to 28
- q_bracket: int32 [2, 1024], replicated, may hold values from 0 to 28
- p_weight: float32 [2, 4, 1024], replicated, may hold values from -0.25 to 1
- q_weight: float32 [2, 4, 1024], replicated, may hold values from -0.25 to 1
- qr_bracket: int32 [2, 1024], replicated, may hold values from 0 to 28
- r_bracket: int32 [2, 1024], replicated, may hold values from 0 to 28
- qr_weight: float32 [2, 4, 1024], replicated, may hold values from -0.25 to 1
- r_weight: float32 [2, 4, 1024], replicated, may hold values from -0.25 to 1
Outputs:
- amplitude: float32 [256, 128, 1024], P(('energy', 'mom')), parts along dimension 0
- component: float32 [256, 128, 1024], P(('energy', 'mom')), parts along dimension 0
There are 2 independent parts, one for each index of `energy`. A program takes and returns all parts, laid end to end along the dimension named above; an argument that names none is the same for every part. Nothing has to cross between parts.
All inputs are finite; a program needn't handle non-finite values.
Results may differ from a plain program's by a relative error of at most 0.0001.
Values sent between devices are 32-bit elements; how exact they have to be, the bound alone decides.
No kernel may reach another device: no remote copies, remote signals or barrier semaphores. Data moves between devices by JAX's collectives and lax.ppermute only.
A program may use at most 128 MiB of HBM per device.

v0:
```python
import jax
import jax.numpy as jnp
from jax import lax
from jax.sharding import PartitionSpec as P

P_SIZE = 32
Q = 32
R = 32
K = 2
ITERS = 2


def spline_matrix(
    first_index, second_index, first_weight, second_weight, first_count, second_count
):
    first_grid = jnp.arange(first_count, dtype=jnp.int32)[None, :] - first_index[:, None]
    second_grid = jnp.arange(second_count, dtype=jnp.int32)[None, :] - second_index[:, None]
    first_rows = jnp.zeros(first_grid.shape, jnp.float32)
    second_rows = jnp.zeros(second_grid.shape, jnp.float32)
    for offset in range(4):
        first_rows = first_rows + jnp.where(
            first_grid == offset, first_weight[offset][:, None], jnp.float32(0.0)
        )
        second_rows = second_rows + jnp.where(
            second_grid == offset, second_weight[offset][:, None], jnp.float32(0.0)
        )
    return (first_rows[:, :, None] * second_rows[:, None, :]).reshape(
        first_index.shape[0], first_count * second_count
    )


def class_mats(couple, row_count, start):
    classes = (start + jnp.arange(row_count, dtype=jnp.int32)) % 4
    select = jax.nn.one_hot(classes, 4, dtype=jnp.float32)
    return jnp.einsum("rc,cmn->rmn", select, couple, precision=lax.Precision.HIGHEST)


def mix(mats, values):
    return jnp.einsum("rmn,rnx->rmx", mats, values, precision=lax.Precision.HIGHEST)


def interp(values, smat):
    return jnp.einsum("rcx,yx->rcy", values, smat, precision=lax.Precision.HIGHEST)


def to_send_one(values, quarter):
    rows = values.shape[0]
    return (
        values.reshape(rows, 4, quarter, P_SIZE, Q)
        .transpose(3, 1, 0, 2, 4)
        .reshape(4 * P_SIZE, rows, quarter * Q)
    )


def from_send_one(arrived, quarter):
    rows = arrived.shape[0]
    return (
        arrived.reshape(rows, R, 4, quarter, Q)
        .transpose(0, 3, 2, 4, 1)
        .reshape(rows, 4 * quarter, Q * R)
    )


def to_send_two(values, quarter):
    rows = values.shape[0]
    return (
        values.reshape(rows, quarter, 4, Q, R)
        .transpose(4, 2, 0, 1, 3)
        .reshape(4 * R, rows, quarter * Q)
    )


def from_send_two(arrived, quarter):
    rows = arrived.shape[0]
    return (
        arrived.reshape(rows, P_SIZE, 4, quarter, Q)
        .transpose(0, 2, 3, 1, 4)
        .reshape(rows, 4 * quarter, P_SIZE * Q)
    )


def shards(
    source,
    green,
    couple_one,
    couple_two,
    p_bracket,
    q_bracket,
    p_weight,
    q_weight,
    qr_bracket,
    r_bracket,
    qr_weight,
    r_weight,
):
    rows_one = source.shape[0]
    rows_two = green.shape[0]
    quarter = source.shape[1] // 4
    here = lax.axis_index("mom")
    first_maps = [
        spline_matrix(p_bracket[k], q_bracket[k], p_weight[k], q_weight[k], P_SIZE, Q)
        for k in range(K)
    ]
    second_maps = [
        spline_matrix(qr_bracket[k], r_bracket[k], qr_weight[k], r_weight[k], Q, R)
        for k in range(K)
    ]
    mats_one = [class_mats(couple_one[k], rows_one, here * rows_one) for k in range(K)]
    mats_two = [class_mats(couple_two[k], rows_two, here * rows_two) for k in range(K)]
    scale = green[:, None, :]
    state = source
    component = None
    for step in range(ITERS):
        one = interp(mix(mats_one[0], state), first_maps[0])
        k = 1
        one = one + interp(mix(mats_one[k], state), first_maps[k])
        arrived = lax.all_to_all(
            to_send_one(one, quarter), "mom", split_axis=0, concat_axis=1, tiled=True
        )
        regrouped = from_send_one(arrived, quarter)
        total = mix(mats_two[0], interp(regrouped, second_maps[0]))
        k = 1
        total = total + mix(mats_two[k], interp(regrouped, second_maps[k]))
        component = scale * total
        returned = lax.all_to_all(
            to_send_two(component, quarter), "mom", split_axis=0, concat_axis=1, tiled=True
        )
        state = source + from_send_two(returned, quarter)
    return (state, component)


def solution(mesh):
    placed = (
        P(("energy", "mom"), None, None),
        P(("energy", "mom"), None),
        P(),
        P(),
        P(),
        P(),
        P(),
        P(),
        P(),
        P(),
        P(),
        P(),
    )
    return jax.shard_map(
        shards,
        mesh=mesh,
        in_specs=placed,
        out_specs=(P(("energy", "mom"), None, None), P(("energy", "mom"), None, None)),
        check_vma=False,
    )
```

profile of v0, /device:TPU:1, one launch (start us, length us, event | category | flops | bytes accessed | tf_op | source)
XLA Modules:
  0.0 923.5 jit_solution(14042595359069601299)
XLA Ops:
  0.6 0.8 fusion.66
  1.4 0.8 fusion.67
  2.2 0.9 fusion.62
  3.2 0.9 fusion.63
  4.1 1.1 fusion.59
  5.2 0.5 fusion.17
  5.7 0.5 fusion.18
  6.3 5.8 fusion.8
  12.2 4.1 fusion.14
  16.4 0.5 broadcast_multiply_fusion.3
  16.9 0.1 select_add_fusion.4
  17.0 0.5 broadcast_multiply_fusion.2
  17.6 14.4 %fusion.68 = f32[8,128,1024]{2,1,0:T(8,128)S(1)} fusion(f32[8,128,1024]{2,1,0:T(8,128)S(1)} %fusion.8, f32[1024,1024,1]{0,1,2:T(8,128)S(1)} %bitcast.165), kind=kOutput, calls=%fused_computation.102 | convolution fusion | flops 12884901888 | bytes 12582912 | tf_op jit(solution)/shard_map/rcx,yx->rcy/dot_general | solution.py:43
  31.9 14.8 %convolution_add_fusion.1 = f32[8,128,1024]{2,1,0:T(8,128)} fusion(f32[8,128,1024]{2,1,0:T(8,128)S(1)} %fusion.68, f32[8,128,1024]{2,1,0:T(8,128)S(1)} %fusion.14, f32[1024,1024,1]{0,1,2:T(8,128)S(1)} %bitcast.156), kind=kOutput, calls=%fused_computation.13 | convolution fusion | flops 12885950464 | bytes 16777216 | tf_op jit(solution)/shard_map/rcx,yx->rcy/dot_general | solution.py:43
  46.8 11.6 %reshape.954 = f32[8,4,32,32,32]{4,3,2,1,0:T(8,128)} reshape(f32[8,128,1024]{2,1,0:T(8,128)} %convolution_add_fusion.1) | data formatting | bytes 8388608 | tf_op jit(solution)/shard_map/reshape | solution.py:49
  58.4 14.3 %copy.127 = f32[8,4,32,32,32]{4,2,0,1,3:T(8,128)} copy(f32[8,4,32,32,32]{4,3,2,1,0:T(8,128)} %reshape.954) | data formatting | bytes 8388608 | tf_op jit(solution)/shard_map/reshape | solution.py:49
  72.7 13.7 %reshape.955 = f32[128,8,1024]{2,1,0:T(8,128)} reshape(f32[32,4,8,32,32]{4,3,2,1,0:T(8,128)} %bitcast.148) | data formatting | bytes 8388608 | tf_op jit(solution)/shard_map/reshape | solution.py:51
  86.4 7.5 all-to-all-start
  94.3 0.5 fusion.16
  94.8 0.5 fusion.19
  95.4 2.5 broadcast_multiply_fusion.1
  97.9 2.6 broadcast_multiply_fusion
  100.5 71.5 %all-to-all-done = f32[128,8,1024]{2,1,0:T(8,128)} async-done(((f32[128,8,1024]{2,1,0:T(8,128)}), f32[128,8,1024]{2,1,0:T(8,128)}, u32[]{:S(2)}, u32[]{:S(2)}) %all-to-all-start) | async-done | bytes 4194336 | tf_op jit(solution)/shard_map/all_to_all | solution.py:117
  172.0 4.8 copy.131
  176.8 11.6 %reshape.956 = f32[8,32,4,32,32]{4,3,2,1,0:T(8,128)} reshape(f32[8,16,8,1024]{3,2,1,0:T(8,128)} %bitcast.158) | data formatting | bytes 8388608 | tf_op jit(solution)/shard_map/reshape | solution.py:58
  188.4 18.9 %copy.53 = f32[8,32,4,32,32]{4,3,2,1,0:T(8,128)} copy(f32[8,32,4,32,32]{3,1,2,4,0:T(8,128)} %bitcast.149) | data formatting | bytes 8388608 | tf_op jit(solution)/shard_map/transpose | solution.py:59
  207.3 13.7 %reshape.957 = f32[8,128,1024]{2,1,0:T(8,128)} reshape(f32[8,32,4,32,32]{4,3,2,1,0:T(8,128)} %copy.53) | data formatting | bytes 8388608 | tf_op jit(solution)/shard_map/reshape | solution.py:60
  221.0 17.2 %fusion.70 = f32[8,128,1024]{2,1,0:T(8,128)S(1)} fusion(f32[8,128,1024]{2,1,0:T(8,128)} %reshape.957, f32[1024,1024,1]{0,1,2:T(8,128)} %bitcast.169), kind=kOutput, calls=%fused_computation.104 | convolution fusion | flops 12884901888 | bytes 12582912 | tf_op jit(solution)/shard_map/rcx,yx->rcy/dot_general | solution.py:43
  238.2 13.4 %fusion.69 = f32[8,128,1024]{2,1,0:T(8,128)S(1)} fusion(f32[8,128,1024]{2,1,0:T(8,128)S(1)} %copy-done.6, f32[1024,1024,1]{0,1,2:T(8,128)S(1)} %bitcast.167), kind=kOutput, calls=%fused_computation.103 | convolution fusion | flops 12884901888 | bytes 12582912 | tf_op jit(solution)/shard_map/rcx,yx->rcy/dot_general | solution.py:43
  251.7 4.2 fusion.4
  255.9 5.2 add_multiply_fusion.1
  261.2 11.6 %reshape.958 = f32[8,32,4,32,32]{4,3,2,1,0:T(8,128)} reshape(f32[8,128,1024]{2,1,0:T(8,128)} %add_multiply_fusion.1) | data formatting | bytes 8388608 | tf_op jit(solution)/shard_map/reshape | solution.py:67
  272.8 20.0 %copy.59 = f32[8,32,4,32,32]{3,1,0,2,4:T(8,128)} copy(f32[8,32,4,32,32]{4,3,2,1,0:T(8,128)} %reshape.958) | data formatting | bytes 8388608 | tf_op jit(solution)/shard_map/reshape | solution.py:67
  292.8 13.7 %reshape.959 = f32[128,8,1024]{2,1,0:T(8,128)} reshape(f32[32,4,8,32,32]{4,3,2,1,0:T(8,128)} %bitcast.150) | data formatting | bytes 8388608 | tf_op jit(solution)/shard_map/reshape | solution.py:69
  306.5 111.9 %all_to_all.60 = f32[128,8,1024]{2,1,0:T(8,128)S(1)} all-to-all(f32[128,8,1024]{2,1,0:T(8,128)} %reshape.959), channel_id=1, replica_groups=mesh['energy'=2,'mom'=16] {'mom'}, dimensions={0} | all-to-all | bytes 8388608 | tf_op jit(solution)/shard_map/all_to_all | solution.py:125
  418.4 2.3 copy.130
  420.7 11.6 %reshape.960 = f32[8,32,4,32,32]{4,3,2,1,0:T(8,128)} reshape(f32[8,16,8,1024]{3,2,1,0:T(8,128)} %bitcast.159) | data formatting | bytes 8388608 | tf_op jit(solution)/shard_map/reshape | solution.py:76
  432.3 18.4 %copy.61 = f32[8,4,32,32,32]{4,3,2,1,0:T(8,128)} copy(f32[8,4,32,32,32]{4,2,1,3,0:T(8,128)} %bitcast.151) | data formatting | bytes 8388608 | tf_op jit(solution)/shard_map/transpose | solution.py:77
  450.8 13.7 %reshape.961 = f32[8,128,1024]{2,1,0:T(8,128)} reshape(f32[8,4,32,32,32]{4,3,2,1,0:T(8,128)} %copy.61) | data formatting | bytes 8388608 | tf_op jit(solution)/shard_map/reshape | solution.py:78
  464.4 6.4 fusion
  470.8 3.9 fusion.2
  474.8 14.2 %fusion.71 = f32[8,128,1024]{2,1,0:T(8,128)S(1)} fusion(f32[8,128,1024]{2,1,0:T(8,128)S(1)} %fusion.2, f32[1024,1024,1]{0,1,2:T(8,128)S(1)} %bitcast.166), kind=kOutput, calls=%fused_computation.105 | convolution fusion | flops 12884901888 | bytes 12582912 | tf_op jit(solution)/shard_map/rcx,yx->rcy/dot_general | solution.py:43
  489.0 14.8 %convolution_add_fusion = f32[8,128,1024]{2,1,0:T(8,128)} fusion(f32[8,128,1024]{2,1,0:T(8,128)S(1)} %fusion.71, f32[8,128,1024]{2,1,0:T(8,128)S(1)} %fusion, f32[1024,1024,1]{0,1,2:T(8,128)S(1)} %bitcast.157), kind=kOutput, calls=%fused_computation.12 | convolution fusion | flops 12885950464 | bytes 16777216 | tf_op jit(solution)/shard_map/rcx,yx->rcy/dot_general | solution.py:43
  503.8 11.6 %reshape.962 = f32[8,4,32,32,32]{4,3,2,1,0:T(8,128)} reshape(f32[8,128,1024]{2,1,0:T(8,128)} %convolution_add_fusion) | data formatting | bytes 8388608 | tf_op jit(solution)/shard_map/reshape | solution.py:49
  515.4 14.3 %copy.126 = f32[8,4,32,32,32]{4,2,0,1,3:T(8,128)} copy(f32[8,4,32,32,32]{4,3,2,1,0:T(8,128)} %reshape.962) | data formatting | bytes 8388608 | tf_op jit(solution)/shard_map/reshape | solution.py:49
  529.7 13.7 %reshape.963 = f32[128,8,1024]{2,1,0:T(8,128)} reshape(f32[32,4,8,32,32]{4,3,2,1,0:T(8,128)} %bitcast.152) | data formatting | bytes 8388608 | tf_op jit(solution)/shard_map/reshape | solution.py:51
  543.4 97.4 %all_to_all.61 = f32[128,8,1024]{2,1,0:T(8,128)S(1)} all-to-all(f32[128,8,1024]{2,1,0:T(8,128)} %reshape.963), channel_id=1, replica_groups=mesh['energy'=2,'mom'=16] {'mom'}, dimensions={0} | all-to-all | bytes 8388608 | tf_op jit(solution)/shard_map/all_to_all | solution.py:117
  640.8 2.3 copy.129
  643.1 11.6 %reshape.964 = f32[8,32,4,32,32]{4,3,2,1,0:T(8,128)} reshape(f32[8,16,8,1024]{3,2,1,0:T(8,128)} %bitcast.160) | data formatting | bytes 8388608 | tf_op jit(solution)/shard_map/reshape | solution.py:58
  654.7 18.9 %copy.68 = f32[8,32,4,32,32]{4,3,2,1,0:T(8,128)} copy(f32[8,32,4,32,32]{3,1,2,4,0:T(8,128)} %bitcast.153) | data formatting | bytes 8388608 | tf_op jit(solution)/shard_map/transpose | solution.py:59
  673.6 13.7 %reshape.965 = f32[8,128,1024]{2,1,0:T(8,128)} reshape(f32[8,32,4,32,32]{4,3,2,1,0:T(8,128)} %copy.68) | data formatting | bytes 8388608 | tf_op jit(solution)/shard_map/reshape | solution.py:60
  687.3 17.2 %fusion.73 = f32[8,128,1024]{2,1,0:T(8,128)S(1)} fusion(f32[8,128,1024]{2,1,0:T(8,128)} %reshape.965, f32[1024,1024,1]{0,1,2:T(8,128)} %bitcast.170), kind=kOutput, calls=%fused_computation.107 | convolution fusion | flops 12884901888 | bytes 12582912 | tf_op jit(solution)/shard_map/rcx,yx->rcy/dot_general | solution.py:43
  704.6 13.4 %fusion.72 = f32[8,128,1024]{2,1,0:T(8,128)S(1)} fusion(f32[8,128,1024]{2,1,0:T(8,128)S(1)} %copy-done.5, f32[1024,1024,1]{0,1,2:T(8,128)S(1)} %bitcast.168), kind=kOutput, calls=%fused_computation.106 | convolution fusion | flops 12884901888 | bytes 12582912 | tf_op jit(solution)/shard_map/rcx,yx->rcy/dot_general | solution.py:43
  718.0 4.2 fusion.6
  722.3 5.2 add_multiply_fusion
  727.5 11.6 %reshape.966 = f32[8,32,4,32,32]{4,3,2,1,0:T(8,128)} reshape(f32[8,128,1024]{2,1,0:T(8,128)} %add_multiply_fusion) | data formatting | bytes 8388608 | tf_op jit(solution)/shard_map/reshape | solution.py:67
  739.1 20.0 %copy.73 = f32[8,32,4,32,32]{3,1,0,2,4:T(8,128)} copy(f32[8,32,4,32,32]{4,3,2,1,0:T(8,128)} %reshape.966) | data formatting | bytes 8388608 | tf_op jit(solution)/shard_map/reshape | solution.py:67
  759.1 13.7 %reshape.967 = f32[128,8,1024]{2,1,0:T(8,128)} reshape(f32[32,4,8,32,32]{4,3,2,1,0:T(8,128)} %bitcast.154) | data formatting | bytes 8388608 | tf_op jit(solution)/shard_map/reshape | solution.py:69
  772.8 97.6 %all_to_all.62 = f32[128,8,1024]{2,1,0:T(8,128)S(1)} all-to-all(f32[128,8,1024]{2,1,0:T(8,128)} %reshape.967), channel_id=1, replica_groups=mesh['energy'=2,'mom'=16] {'mom'}, dimensions={0} | all-to-all | bytes 8388608 | tf_op jit(solution)/shard_map/all_to_all | solution.py:125
  870.4 2.3 copy.128
  872.7 11.6 %reshape.968 = f32[8,32,4,32,32]{4,3,2,1,0:T(8,128)} reshape(f32[8,16,8,1024]{3,2,1,0:T(8,128)} %bitcast.161) | data formatting | bytes 8388608 | tf_op jit(solution)/shard_map/reshape | solution.py:76
  884.3 18.4 %copy.75 = f32[8,4,32,32,32]{4,3,2,1,0:T(8,128)} copy(f32[8,4,32,32,32]{4,2,1,3,0:T(8,128)} %bitcast.155) | data formatting | bytes 8388608 | tf_op jit(solution)/shard_map/transpose | solution.py:77
  902.8 13.7 %reshape.969 = f32[8,128,1024]{2,1,0:T(8,128)} reshape(f32[8,4,32,32,32]{4,3,2,1,0:T(8,128)} %copy.75) | data formatting | bytes 8388608 | tf_op jit(solution)/shard_map/reshape | solution.py:78
  916.4 6.8 add.250
  (43 shorter events, 0.5 us)
Async XLA Ops:
  6.3 5.8 copy-start
  16.9 15.0 %copy-start.7 = (f32[1024,32,32]{0,2,1:T(8,128)}, f32[1024,32,32]{0,2,1:T(8,128)S(1)}, u32[]{:S(2)}) copy-start(f32[1024,32,32]{0,2,1:T(8,128)S(1)} %broadcast_multiply_fusion.3) | copy-start | bytes 12582916
  17.5 14.4 %copy-start.3 = (f32[1024,32,32]{0,2,1:T(8,128)}, f32[1024,32,32]{0,2,1:T(8,128)S(1)}, u32[]{:S(2)}) copy-start(f32[1024,32,32]{0,2,1:T(8,128)S(1)} %broadcast_multiply_fusion.2) | copy-start | bytes 12582916
  86.3 7.5 copy-start.15
  86.3 7.5 copy-start.16
  86.3 7.6 copy-start.13
  86.3 7.6 copy-start.14
  86.4 7.9 copy-start.11
  86.4 85.6 %all-to-all-start = ((f32[128,8,1024]{2,1,0:T(8,128)}), f32[128,8,1024]{2,1,0:T(8,128)}, u32[]{:S(2)}, u32[]{:S(2)}) async-start(f32[128,8,1024]{2,1,0:T(8,128)} %reshape.955), calls=%async_computation | async-start | bytes 8388608 | tf_op jit(solution)/shard_map/all_to_all | solution.py:117
  221.0 17.2 %copy-start.6 = (f32[8,128,1024]{2,1,0:T(8,128)S(1)}, f32[8,128,1024]{2,1,0:T(8,128)}, u32[]{:S(2)}) copy-start(f32[8,128,1024]{2,1,0:T(8,128)} %reshape.957) | copy-start | bytes 12582916
  221.0 17.3 %copy-start.9 = (f32[1024,32,32]{0,2,1:T(8,128)S(1)}, f32[1024,32,32]{0,2,1:T(8,128)}, u32[]{:S(2)}) copy-start(f32[1024,32,32]{0,2,1:T(8,128)} %broadcast_multiply_fusion.1) | copy-start | bytes 12582916
  251.7 4.3 copy-start.12
  464.4 6.4 copy-start.1
  464.4 6.4 copy-start.2
  470.8 4.0 copy-start.8
  474.8 14.2 %copy-start.4 = (f32[1024,32,32]{0,2,1:T(8,128)S(1)}, f32[1024,32,32]{0,2,1:T(8,128)}, u32[]{:S(2)}) copy-start(f32[1024,32,32]{0,2,1:T(8,128)} %copy-done.3) | copy-start | bytes 12582916
  687.3 17.2 %copy-start.5 = (f32[8,128,1024]{2,1,0:T(8,128)S(1)}, f32[8,128,1024]{2,1,0:T(8,128)}, u32[]{:S(2)}) copy-start(f32[8,128,1024]{2,1,0:T(8,128)} %reshape.965) | copy-start | bytes 12582916
  687.3 17.3 %copy-start.10 = (f32[1024,32,32]{0,2,1:T(8,128)S(1)}, f32[1024,32,32]{0,2,1:T(8,128)}, u32[]{:S(2)}) copy-start(f32[1024,32,32]{0,2,1:T(8,128)} %broadcast_multiply_fusion.1) | copy-start | bytes 12582916
where the time goes:
time: 932 us; the launch traced here: 923 us
  local copies, waits for them, and re-layouts  362 us (39%)
  blocking collectives  307 us (33%)
  matrix products  161 us (17%)
  waiting for transfers between devices  71.5 us (8%)
  other arithmetic  13.5 us (1%)
    all_to_all x2, blocking collectives, shards(): lax.all_to_all(to_send_two(component, quarter), 'mom', split_axis=0, conc...  210 us
    dot_general x8, matrix products, interp(): jnp.einsum('rcx,yx->rcy', values, smat, precision=lax.Precision.HIGHEST)  120 us
    all_to_all x1, blocking collectives, shards(): lax.all_to_all(to_send_one(one, quarter), 'mom', split_axis=0, concat_axi...  97.4 us
    all_to_all x1, waiting for transfers between devices, shards(): lax.all_to_all(to_send_one(one, quarter), 'mom', split_axis=0, concat_axi...  71.5 us
    reshape x4, local copies, waits for them, and re-layouts, to_send_two(): values.reshape(rows, quarter, 4, Q, R).transpose(4, 2, 0, 1, 3)  63.2 us
    reshape x4, local copies, waits for them, and re-layouts, to_send_one(): values.reshape(rows, 4, quarter, P_SIZE, Q).transpose(3, 1, 0, 2, 4)  51.8 us
    dot_general x8, matrix products, mix(): jnp.einsum('rmn,rnx->rmx', mats, values, precision=lax.Precision.HIGHEST)  39.1 us
    transpose x2, local copies, waits for them, and re-layouts, from_send_one(): return arrived.reshape(rows, R, 4, quarter, Q).transpose(0, 3, 2, 4, 1).r...  37.8 us
  transfers between devices with their start and end apart: 1, of which 1 were waited for; matrix products, arithmetic and copies ran while one was open for 1% of the time, Pallas kernels for 0%

commit v1 on v0

--- a/solution.py
+++ b/solution.py
@@ -114,8 +114,14 @@
         one = interp(mix(mats_one[0], state), first_maps[0])
         k = 1
         one = one + interp(mix(mats_one[k], state), first_maps[k])
-        arrived = lax.all_to_all(
-            to_send_one(one, quarter), "mom", split_axis=0, concat_axis=1, tiled=True
+        arrived = jnp.concatenate(
+            lax.all_to_all(
+                jnp.stack(jnp.split(to_send_one(one, quarter), lax.axis_size("mom"), axis=0)),
+                "mom",
+                0,
+                0,
+            ),
+            axis=1,
         )
         regrouped = from_send_one(arrived, quarter)
         total = mix(mats_two[0], interp(regrouped, second_maps[0]))

time: 932 us -> 1020 us (1.094)
  local copies, waits for them, and re-layouts: 362 us -> 445 us
    another operation x0 -> x36, local copies, waits for them, and re-layouts: none -> 93.1 us  [the longest x34 69.9 us: shards(): jnp.stack(jnp.split(to_send_one(one, quarter), lax.axis_size('mom'), axis...]
    reshape x4 -> x2, local copies, waits for them, and re-layouts: 50.6 us -> 7.11 us  [shards(): jnp.concatenate(lax.all_to_all(jnp.stack(jnp.split(to_send_one(one, quart...]
    unnamed x34 -> x84, local copies, waits for them, and re-layouts: 0.07 us -> 39 us
    split x0 -> x2, local copies, waits for them, and re-layouts: none -> 10.5 us  [shards(): jnp.split(to_send_one(one, quarter), lax.axis_size('mom'), axis=0)]
where the time goes in v1:
time: 1020 us; the launch traced here: 1010 us
  local copies, waits for them, and re-layouts  445 us (44%)
  blocking collectives  307 us (30%)
  matrix products  160 us (16%)
  waiting for transfers between devices  71.3 us (7%)
  other arithmetic  13.5 us (1%)
    all_to_all x2, blocking collectives, shards(): lax.all_to_all(to_send_two(component, quarter), 'mom', split_axis=0, conc...  210 us
    dot_general x8, matrix products, interp(): jnp.einsum('rcx,yx->rcy', values, smat, precision=lax.Precision.HIGHEST)  119 us
    all_to_all x1, blocking collectives, shards(): lax.all_to_all(jnp.stack(jnp.split(to_send_one(one, quarter), lax.axis_si...  97.6 us
    all_to_all x1, waiting for transfers between devices, shards(): lax.all_to_all(jnp.stack(jnp.split(to_send_one(one, quarter), lax.axis_si...  71.3 us
    another operation x34, local copies, waits for them, and re-layouts, shards(): jnp.stack(jnp.split(to_send_one(one, quarter), lax.axis_size('mom'), axis...  69.9 us
    reshape x4, local copies, waits for them, and re-layouts, to_send_two(): values.reshape(rows, quarter, 4, Q, R).transpose(4, 2, 0, 1, 3)  63.3 us
    reshape x4, local copies, waits for them, and re-layouts, to_send_one(): values.reshape(rows, 4, quarter, P_SIZE, Q).transpose(3, 1, 0, 2, 4)  42.6 us
    unnamed x84, local copies, waits for them, and re-layouts  39 us
  transfers between devices with their start and end apart: 1, of which 1 were waited for; matrix products, arithmetic and copies ran while one was open for 1% of the time, Pallas kernels for 0%

profile of v1, /device:TPU:1, one launch (start us, length us, event | category | flops | bytes accessed | tf_op | source)
XLA Modules:
  0.0 1006.2 jit_solution(8085703493979798703)
XLA Ops:
  6.3 5.7 fusion.8
  12.0 4.1 fusion.14
  16.8 14.0 %fusion.70 = f32[8,128,1024]{2,1,0:T(8,128)S(1)} fusion(f32[8,128,1024]{2,1,0:T(8,128)S(1)} %fusion.8, f32[1024,1024,1]{0,1,2:T(8,128)S(1)} %bitcast.217), kind=kOutput, calls=%fused_computation.134 | convolution fusion | flops 12884901888 | bytes 12582912 | tf_op jit(solution)/shard_map/rcx,yx->rcy/dot_general | solution.py:43
  33.4 14.8 %convolution_add_fusion.1 = f32[8,128,1024]{2,1,0:T(8,128)} fusion(f32[8,128,1024]{2,1,0:T(8,128)S(1)} %fusion.70, f32[8,128,1024]{2,1,0:T(8,128)S(1)} %fusion.14, f32[1024,1024,1]{0,1,2:T(8,128)S(1)} %bitcast.210), kind=kOutput, calls=%fused_computation.11 | convolution fusion | flops 12885950464 | bytes 16777216 | tf_op jit(solution)/shard_map/rcx,yx->rcy/dot_general | solution.py:43
  48.2 11.6 %reshape.1012 = f32[8,4,32,32,32]{4,3,2,1,0:T(8,128)} reshape(f32[8,128,1024]{2,1,0:T(8,128)} %convolution_add_fusion.1) | data formatting | bytes 8388608 | tf_op jit(solution)/shard_map/reshape | solution.py:49
  59.8 9.8 copy.125
  69.6 5.3 fusion.59
  77.3 2.4 stack.103
  89.4 2.4 stack.108
  91.8 2.4 stack.109
  101.5 2.4 stack.113
  103.9 2.4 stack.114
  106.4 2.5 stack.115
  128.4 7.8 all-to-all-start
  137.7 2.5 broadcast_multiply_fusion.1
  140.2 2.6 broadcast_multiply_fusion
  142.8 71.3 %all-to-all-done = f32[16,8,8,1024]{3,2,1,0:T(8,128)} async-done(((f32[16,8,8,1024]{3,2,1,0:T(8,128)}), f32[16,8,8,1024]{3,2,1,0:T(8,128)}, u32[]{:S(2)}, u32[]{:S(2)}) %all-to-all-start) | async-done | bytes 4194336 | tf_op jit(solution)/shard_map/all_to_all | solution.py:118
  214.1 4.8 copy.52
  218.9 11.6 %reshape_reshape.6 = f32[8,32,4,32,32]{4,3,2,1,0:T(8,128)} reshape(f32[8,16,8,1024]{3,2,1,0:T(8,128)} %copy.52) | data formatting | bytes 8388608 | tf_op jit(solution)/shard_map/reshape;reshape | solution.py:58
  230.6 18.9 %copy.53 = f32[8,32,4,32,32]{4,3,2,1,0:T(8,128)} copy(f32[8,32,4,32,32]{3,1,2,4,0:T(8,128)} %bitcast.202) | data formatting | bytes 8388608 | tf_op jit(solution)/shard_map/transpose | solution.py:59
  249.4 13.7 %reshape.1014 = f32[8,128,1024]{2,1,0:T(8,128)} reshape(f32[8,32,4,32,32]{4,3,2,1,0:T(8,128)} %copy.53) | data formatting | bytes 8388608 | tf_op jit(solution)/shard_map/reshape | solution.py:60
  263.1 17.2 %fusion.71 = f32[8,128,1024]{2,1,0:T(8,128)S(1)} fusion(f32[8,128,1024]{2,1,0:T(8,128)} %reshape.1014, f32[1024,1024,1]{0,1,2:T(8,128)} %bitcast.219), kind=kOutput, calls=%fused_computation.135 | convolution fusion | flops 12884901888 | bytes 12582912 | tf_op jit(solution)/shard_map/rcx,yx->rcy/dot_general | solution.py:43
  280.4 13.4 %fusion.72 = f32[8,128,1024]{2,1,0:T(8,128)S(1)} fusion(f32[8,128,1024]{2,1,0:T(8,128)S(1)} %copy-done.6, f32[1024,1024,1]{0,1,2:T(8,128)S(1)} %bitcast.222), kind=kOutput, calls=%fused_computation.136 | convolution fusion | flops 12884901888 | bytes 12582912 | tf_op jit(solution)/shard_map/rcx,yx->rcy/dot_general | solution.py:43
  293.8 4.2 fusion.4
  298.1 5.2 add_multiply_fusion.1
  303.3 11.6 %reshape.1015 = f32[8,32,4,32,32]{4,3,2,1,0:T(8,128)} reshape(f32[8,128,1024]{2,1,0:T(8,128)} %add_multiply_fusion.1) | data formatting | bytes 8388608 | tf_op jit(solution)/shard_map/reshape | solution.py:67
  314.9 20.0 %copy.59 = f32[8,32,4,32,32]{3,1,0,2,4:T(8,128)} copy(f32[8,32,4,32,32]{4,3,2,1,0:T(8,128)} %reshape.1015) | data formatting | bytes 8388608 | tf_op jit(solution)/shard_map/reshape | solution.py:67
  334.9 13.7 %reshape.1016 = f32[128,8,1024]{2,1,0:T(8,128)} reshape(f32[32,4,8,32,32]{4,3,2,1,0:T(8,128)} %bitcast.203) | data formatting | bytes 8388608 | tf_op jit(solution)/shard_map/reshape | solution.py:69
  348.6 111.9 %all_to_all.40 = f32[128,8,1024]{2,1,0:T(8,128)S(1)} all-to-all(f32[128,8,1024]{2,1,0:T(8,128)} %reshape.1016), channel_id=1, replica_groups=mesh['energy'=2,'mom'=16] {'mom'}, dimensions={0} | all-to-all | bytes 8388608 | tf_op jit(solution)/shard_map/all_to_all | solution.py:131
  462.8 11.6 %reshape.1017 = f32[8,32,4,32,32]{4,3,2,1,0:T(8,128)} reshape(f32[8,16,8,1024]{3,2,1,0:T(8,128)} %bitcast.212) | data formatting | bytes 8388608 | tf_op jit(solution)/shard_map/reshape | solution.py:76
  474.4 18.5 %copy.61 = f32[8,4,32,32,32]{4,3,2,1,0:T(8,128)} copy(f32[8,4,32,32,32]{4,2,1,3,0:T(8,128)} %bitcast.204) | data formatting | bytes 8388608 | tf_op jit(solution)/shard_map/transpose | solution.py:77
  492.9 13.7 %reshape.1018 = f32[8,128,1024]{2,1,0:T(8,128)} reshape(f32[8,4,32,32,32]{4,3,2,1,0:T(8,128)} %copy.61) | data formatting | bytes 8388608 | tf_op jit(solution)/shard_map/reshape | solution.py:78
  506.6 6.4 fusion.2
  513.0 3.9 fusion
  516.9 14.2 %fusion.73 = f32[8,128,1024]{2,1,0:T(8,128)S(1)} fusion(f32[8,128,1024]{2,1,0:T(8,128)S(1)} %fusion.2, f32[1024,1024,1]{0,1,2:T(8,128)S(1)} %bitcast.218), kind=kOutput, calls=%fused_computation.137 | convolution fusion | flops 12884901888 | bytes 12582912 | tf_op jit(solution)/shard_map/rcx,yx->rcy/dot_general | solution.py:43
  531.1 14.8 %convolution_add_fusion = f32[8,128,1024]{2,1,0:T(8,128)} fusion(f32[8,128,1024]{2,1,0:T(8,128)S(1)} %fusion.73, f32[8,128,1024]{2,1,0:T(8,128)S(1)} %fusion, f32[1024,1024,1]{0,1,2:T(8,128)S(1)} %bitcast.211), kind=kOutput, calls=%fused_computation.10 | convolution fusion | flops 12885950464 | bytes 16777216 | tf_op jit(solution)/shard_map/rcx,yx->rcy/dot_general | solution.py:43
  546.0 11.6 %reshape.1019 = f32[8,4,32,32,32]{4,3,2,1,0:T(8,128)} reshape(f32[8,128,1024]{2,1,0:T(8,128)} %convolution_add_fusion) | data formatting | bytes 8388608 | tf_op jit(solution)/shard_map/reshape | solution.py:49
  557.6 9.6 copy.124
  567.1 5.3 fusion.58
  574.8 2.4 stack.120
  577.3 2.4 stack.121
  589.3 2.4 stack.126
  591.8 2.4 stack.127
  594.2 2.4 stack.128
  596.6 2.5 stack.129
  599.1 2.4 stack.130
  601.5 2.4 stack.131
  604.0 2.4 stack.132
  625.9 97.6 %all_to_all.41 = f32[16,8,8,1024]{3,2,1,0:T(8,128)S(1)} all-to-all(f32[16,8,8,1024]{3,2,1,0:T(8,128)} %constant_dynamic-update-slice_fusion.16), channel_id=1, replica_groups=mesh['energy'=2,'mom'=16] {'mom'}, dimensions={0} | all-to-all | bytes 8388608 | tf_op jit(solution)/shard_map/all_to_all | solution.py:118
  725.8 11.6 %reshape_reshape.7 = f32[8,32,4,32,32]{4,3,2,1,0:T(8,128)} reshape(f32[8,16,8,1024]{3,2,1,0:T(8,128)} %copy.67) | data formatting | bytes 8388608 | tf_op jit(solution)/shard_map/reshape;reshape | solution.py:58
  737.5 18.9 %copy.68 = f32[8,32,4,32,32]{4,3,2,1,0:T(8,128)} copy(f32[8,32,4,32,32]{3,1,2,4,0:T(8,128)} %bitcast.205) | data formatting | bytes 8388608 | tf_op jit(solution)/shard_map/transpose | solution.py:59
  756.3 13.7 %reshape.1021 = f32[8,128,1024]{2,1,0:T(8,128)} reshape(f32[8,32,4,32,32]{4,3,2,1,0:T(8,128)} %copy.68) | data formatting | bytes 8388608 | tf_op jit(solution)/shard_map/reshape | solution.py:60
  770.0 17.4 %fusion.75 = f32[8,128,1024]{2,1,0:T(8,128)S(1)} fusion(f32[8,128,1024]{2,1,0:T(8,128)} %reshape.1021, f32[1024,1024,1]{0,1,2:T(8,128)} %bitcast.221), kind=kOutput, calls=%fused_computation.139 | convolution fusion | flops 12884901888 | bytes 12582912 | tf_op jit(solution)/shard_map/rcx,yx->rcy/dot_general | solution.py:43
  787.5 13.4 %fusion.74 = f32[8,128,1024]{2,1,0:T(8,128)S(1)} fusion(f32[8,128,1024]{2,1,0:T(8,128)S(1)} %copy-done.5, f32[1024,1024,1]{0,1,2:T(8,128)S(1)} %bitcast.220), kind=kOutput, calls=%fused_computation.138 | convolution fusion | flops 12884901888 | bytes 12582912 | tf_op jit(solution)/shard_map/rcx,yx->rcy/dot_general | solution.py:43
  800.9 4.0 fusion.6
  804.9 5.2 add_multiply_fusion
  810.1 11.6 %reshape.1022 = f32[8,32,4,32,32]{4,3,2,1,0:T(8,128)} reshape(f32[8,128,1024]{2,1,0:T(8,128)} %add_multiply_fusion) | data formatting | bytes 8388608 | tf_op jit(solution)/shard_map/reshape | solution.py:67
  821.8 20.0 %copy.73 = f32[8,32,4,32,32]{3,1,0,2,4:T(8,128)} copy(f32[8,32,4,32,32]{4,3,2,1,0:T(8,128)} %reshape.1022) | data formatting | bytes 8388608 | tf_op jit(solution)/shard_map/reshape | solution.py:67
  841.8 13.7 %reshape.1023 = f32[128,8,1024]{2,1,0:T(8,128)} reshape(f32[32,4,8,32,32]{4,3,2,1,0:T(8,128)} %bitcast.206) | data formatting | bytes 8388608 | tf_op jit(solution)/shard_map/reshape | solution.py:69
  855.4 97.6 %all_to_all.42 = f32[128,8,1024]{2,1,0:T(8,128)S(1)} all-to-all(f32[128,8,1024]{2,1,0:T(8,128)} %reshape.1023), channel_id=1, replica_groups=mesh['energy'=2,'mom'=16] {'mom'}, dimensions={0} | all-to-all | bytes 8388608 | tf_op jit(solution)/shard_map/all_to_all | solution.py:131
  955.4 11.6 %reshape.1024 = f32[8,32,4,32,32]{4,3,2,1,0:T(8,128)} reshape(f32[8,16,8,1024]{3,2,1,0:T(8,128)} %bitcast.213) | data formatting | bytes 8388608 | tf_op jit(solution)/shard_map/reshape | solution.py:76
  967.0 18.5 %copy.75 = f32[8,4,32,32,32]{4,3,2,1,0:T(8,128)} copy(f32[8,4,32,32,32]{4,2,1,3,0:T(8,128)} %bitcast.207) | data formatting | bytes 8388608 | tf_op jit(solution)/shard_map/transpose | solution.py:77
  985.5 13.7 %reshape.1025 = f32[8,128,1024]{2,1,0:T(8,128)} reshape(f32[8,4,32,32,32]{4,3,2,1,0:T(8,128)} %copy.75) | data formatting | bytes 8388608 | tf_op jit(solution)/shard_map/reshape | solution.py:78
  999.1 6.8 add.250
  (127 shorter events, 87.6 us)
Async XLA Ops:
  6.3 5.7 copy-start
  16.8 14.0 %copy-start.7 = (f32[1024,32,32]{0,2,1:T(8,128)}, f32[1024,32,32]{0,2,1:T(8,128)S(1)}, u32[]{:S(2)}) copy-start(f32[1024,32,32]{0,2,1:T(8,128)S(1)} %broadcast_multiply_fusion.3) | copy-start | bytes 12582916
  31.4 2.0 copy-start.3
  109.3 15.4 %copy-start.15 = (f32[1,8,8,1024]{3,2,1,0:T(8,128)S(1)}, f32[1,8,8,1024]{3,2,1,0:T(8,128)}, u32[]{:S(2)}) copy-start(f32[1,8,8,1024]{3,2,1,0:T(8,128)} %stack.113) | copy-start | bytes 786436
  109.3 16.1 %copy-start.13 = (f32[1,8,8,1024]{3,2,1,0:T(8,128)S(1)}, f32[1,8,8,1024]{3,2,1,0:T(8,128)}, u32[]{:S(2)}) copy-start(f32[1,8,8,1024]{3,2,1,0:T(8,128)} %stack.114) | copy-start | bytes 786436
  109.3 16.8 %copy-start.11 = (f32[1,8,8,1024]{3,2,1,0:T(8,128)S(1)}, f32[1,8,8,1024]{3,2,1,0:T(8,128)}, u32[]{:S(2)}) copy-start(f32[1,8,8,1024]{3,2,1,0:T(8,128)} %stack.115) | copy-start | bytes 786436
  109.8 13.4 %copy-start.19 = (f32[1,8,8,1024]{3,2,1,0:T(8,128)S(1)}, f32[1,8,8,1024]{3,2,1,0:T(8,128)}, u32[]{:S(2)}) copy-start(f32[1,8,8,1024]{3,2,1,0:T(8,128)} %stack.111) | copy-start | bytes 786436
  109.8 14.2 %copy-start.17 = (f32[1,8,8,1024]{3,2,1,0:T(8,128)S(1)}, f32[1,8,8,1024]{3,2,1,0:T(8,128)}, u32[]{:S(2)}) copy-start(f32[1,8,8,1024]{3,2,1,0:T(8,128)} %stack.112) | copy-start | bytes 786436
  128.3 7.8 copy-start.25
  128.3 7.9 copy-start.26
  128.3 7.9 copy-start.23
  128.3 7.9 copy-start.24
  128.3 8.2 copy-start.21
  128.4 85.8 %all-to-all-start = ((f32[16,8,8,1024]{3,2,1,0:T(8,128)}), f32[16,8,8,1024]{3,2,1,0:T(8,128)}, u32[]{:S(2)}, u32[]{:S(2)}) async-start(f32[16,8,8,1024]{3,2,1,0:T(8,128)} %constant_dynamic-update-slice_fusion), calls=%async_computation | async-start | bytes 8388608 | tf_op jit(solution)/shard_map/all_to_all | solution.py:118
  263.1 17.2 %copy-start.6 = (f32[8,128,1024]{2,1,0:T(8,128)S(1)}, f32[8,128,1024]{2,1,0:T(8,128)}, u32[]{:S(2)}) copy-start(f32[8,128,1024]{2,1,0:T(8,128)} %reshape.1014) | copy-start | bytes 12582916
  263.1 17.3 %copy-start.10 = (f32[1024,32,32]{0,2,1:T(8,128)S(1)}, f32[1024,32,32]{0,2,1:T(8,128)}, u32[]{:S(2)}) copy-start(f32[1024,32,32]{0,2,1:T(8,128)} %broadcast_multiply_fusion) | copy-start | bytes 12582916
  293.8 4.3 copy-start.22
  506.6 6.4 copy-start.1
  506.6 6.4 copy-start.2
  513.0 4.0 copy-start.8
  516.9 14.2 %copy-start.4 = (f32[1024,32,32]{0,2,1:T(8,128)S(1)}, f32[1024,32,32]{0,2,1:T(8,128)}, u32[]{:S(2)}) copy-start(f32[1024,32,32]{0,2,1:T(8,128)} %copy-done.3) | copy-start | bytes 12582916
  606.9 15.4 %copy-start.16 = (f32[1,8,8,1024]{3,2,1,0:T(8,128)S(1)}, f32[1,8,8,1024]{3,2,1,0:T(8,128)}, u32[]{:S(2)}) copy-start(f32[1,8,8,1024]{3,2,1,0:T(8,128)} %stack.130) | copy-start | bytes 786436
  606.9 16.1 %copy-start.14 = (f32[1,8,8,1024]{3,2,1,0:T(8,128)S(1)}, f32[1,8,8,1024]{3,2,1,0:T(8,128)}, u32[]{:S(2)}) copy-start(f32[1,8,8,1024]{3,2,1,0:T(8,128)} %stack.131) | copy-start | bytes 786436
  606.9 16.8 %copy-start.12 = (f32[1,8,8,1024]{3,2,1,0:T(8,128)S(1)}, f32[1,8,8,1024]{3,2,1,0:T(8,128)}, u32[]{:S(2)}) copy-start(f32[1,8,8,1024]{3,2,1,0:T(8,128)} %stack.132) | copy-start | bytes 786436
  607.4 13.4 %copy-start.20 = (f32[1,8,8,1024]{3,2,1,0:T(8,128)S(1)}, f32[1,8,8,1024]{3,2,1,0:T(8,128)}, u32[]{:S(2)}) copy-start(f32[1,8,8,1024]{3,2,1,0:T(8,128)} %stack.128) | copy-start | bytes 786436
  607.4 14.2 %copy-start.18 = (f32[1,8,8,1024]{3,2,1,0:T(8,128)S(1)}, f32[1,8,8,1024]{3,2,1,0:T(8,128)}, u32[]{:S(2)}) copy-start(f32[1,8,8,1024]{3,2,1,0:T(8,128)} %stack.129) | copy-start | bytes 786436
  770.0 17.4 %copy-start.5 = (f32[8,128,1024]{2,1,0:T(8,128)S(1)}, f32[8,128,1024]{2,1,0:T(8,128)}, u32[]{:S(2)}) copy-start(f32[8,128,1024]{2,1,0:T(8,128)} %reshape.1021) | copy-start | bytes 12582916
  770.0 17.4 %copy-start.9 = (f32[1024,32,32]{0,2,1:T(8,128)S(1)}, f32[1024,32,32]{0,2,1:T(8,128)}, u32[]{:S(2)}) copy-start(f32[1024,32,32]{0,2,1:T(8,128)} %broadcast_multiply_fusion.1) | copy-start | bytes 12582916
